TPU v7x, 512 devices: a whole 4x8x8 slice. The times are simulated.
512 devices in a mesh: lat: 16 (over z, x_hi), lon: 32 (over y, x_lo, core).
Axes of the slice: x: 4 (x_hi: 2, x_lo: 2; x = x_hi * 2 + x_lo), y: 8, z: 8, core: 2. Of those that a mesh axis runs over, the one named last changes fastest.
Arguments:
- frame: bfloat16 [256, 512, 256], P('lat', 'lon'), may hold values from -64 to 64
- weight_qkv: bfloat16 [256, 768], replicated, may hold values from -0.375 to 0.375
- weight_proj: bfloat16 [256, 256], replicated, may hold values from -0.375 to 0.375
- gain_attn: float32 [256], replicated, may hold values from 0.5 to 1.5
- weight_up: bfloat16 [256, 1024], replicated, may hold values from -0.375 to 0.375
- weight_down: bfloat16 [1024, 256], replicated, may hold values from -0.1875 to 0.1875
- gain_mlp: float32 [256], replicated, may hold values from 0.5 to 1.5
- cotangent: bfloat16 [256, 512, 256], P('lat', 'lon'), may hold values from -6 to 6
Outputs:
- block_out: bfloat16 [256, 512, 256], P('lat', 'lon')
- grad_frame: bfloat16 [256, 512, 256], P('lat', 'lon')
- grad_qkv: bfloat16 [256, 768], replicated
- grad_proj: bfloat16 [256, 256], replicated
- grad_up: bfloat16 [256, 1024], replicated
- grad_down: bfloat16 [1024, 256], replicated
- grad_gain_attn: float32 [256], replicated
- grad_gain_mlp: float32 [256], replicated
All inputs are finite; a program needn't handle non-finite values.
Results may differ from a plain program's by a relative error of at most 0.012.
The roundings to bfloat16 on the way count: a program that leaves them out, or rounds other values in their place, can miss the bound.
Values may be sent and summed in bfloat16 or wider, within the bound.
No kernel may reach another device: no remote copies, remote signals or barrier semaphores. Data moves between devices by JAX's collectives and lax.ppermute only.
A program may use at most 128 MiB of HBM per device.

v0:
```python
import jax
import jax.numpy as jnp
from jax import lax
from jax.sharding import PartitionSpec as P

HEADS = 8
RADIUS = 6
epsilon = 1e-06
cubic_term = 0.044715
gelu_root = 0.7978845608028654
negative_big = -1e30


def padded_2(x, sides, width, wrap):
    for axis, dim in sides:
        devices, length = (lax.axis_size(axis), x.shape[dim])
        up = [(i, (i + 1) % devices) for i in range(devices if wrap else devices - 1)]
        down = [(j, i) for i, j in up]
        last = lax.slice_in_dim(x, length - width, length, axis=dim)
        first = lax.slice_in_dim(x, 0, width, axis=dim)
        before = lax.ppermute(last, axis, up)
        after = lax.ppermute(first, axis, down)
        x = jnp.concatenate([before, x, after], axis=dim)
    return x


def gelu_pair(upward):
    tangent = jnp.tanh(gelu_root * (upward + cubic_term * upward * upward * upward))
    activated = 0.5 * upward * (1.0 + tangent)
    derivative = 0.5 * (1.0 + tangent) + 0.5 * upward * (1.0 - tangent * tangent) * gelu_root * (
        1.0 + 3.0 * cubic_term * upward * upward
    )
    return (activated, derivative)


def rms_factor(field):
    return lax.rsqrt(jnp.mean(field * field, axis=-1, keepdims=True) + epsilon)


def norm_backward(incoming, field, factor):
    mean_term = jnp.mean(incoming * field, axis=-1, keepdims=True)
    return factor * (incoming - field * factor * factor * mean_term)


def contract_rows(left, right):
    return lax.dot_general(
        left, right, (((0,), (0,)), ((), ())), preferred_element_type=jnp.float32
    )


def contract_cols(left, right):
    return lax.dot_general(
        left, right, (((1,), (1,)), ((), ())), preferred_element_type=jnp.float32
    )


def row_strips(padded, rows, span):
    return jnp.stack(
        [lax.slice_in_dim(padded, offset, offset + rows, axis=0) for offset in range(span)], axis=1
    )


def unstrip(strip_sum, rows, span):
    total = jnp.zeros((rows + span - 1,) + strip_sum.shape[2:], strip_sum.dtype)
    for offset in range(span):
        total = total.at[offset : offset + rows].add(strip_sum[:, offset])
    return total


def fold_rims(field, axis, length, radius):
    middle = lax.slice_in_dim(field, 2 * radius, 2 * radius + length, axis=axis)
    front = lax.slice_in_dim(field, 0, radius, axis=axis)
    back = lax.slice_in_dim(field, length + 3 * radius, length + 4 * radius, axis=axis)
    widths_front = [(0, 0)] * field.ndim
    widths_front[axis] = (0, length - radius)
    widths_back = [(0, 0)] * field.ndim
    widths_back[axis] = (length - radius, 0)
    return middle + jnp.pad(front, widths_front) + jnp.pad(back, widths_back)


def band_strips(padded, rows, span, heads):
    strips = row_strips(padded, rows, span)
    return strips.reshape(rows, span * padded.shape[1], heads, padded.shape[2] // heads)


def on_device(
    frame, weight_qkv, weight_proj, gain_attn, weight_up, weight_down, gain_mlp, cotangent
):
    lat_rows, lon_cols, width = frame.shape
    heads = HEADS
    head_size = width // heads
    radius = RADIUS
    span = 2 * radius + 1
    head_scale = head_size ** (-0.5)
    pad_rows = lat_rows + 2 * radius
    pad_cols = lon_cols + 2 * radius
    band = span * pad_cols
    local_tokens = lat_rows * lon_cols
    lat_total = lat_rows * lax.axis_size("lat")
    tokens_all = lat_total * lon_cols * lax.axis_size("lon")
    grad_scale = tokens_all ** (-0.5)
    lat_first = lax.axis_index("lat") * lat_rows
    row_global = lat_first + jnp.arange(lat_rows)[:, None] + jnp.arange(span)[None, :] - radius
    row_ok = (row_global >= 0) & (row_global < lat_total)
    col_gap = jnp.arange(pad_cols)[None, :] - radius - jnp.arange(lon_cols)[:, None]
    near = jnp.abs(col_gap) <= radius
    valid = (row_ok[:, None, :, None] & near[None, :, None, :]).reshape(lat_rows, 1, lon_cols, band)
    flat = frame.reshape(local_tokens, width)
    projected = jnp.dot(flat, weight_qkv, preferred_element_type=jnp.float32).astype(jnp.bfloat16)
    queries = projected[:, :width]
    pairs = projected[:, width:].reshape(lat_rows, lon_cols, 2 * width)
    widened = padded_2(pairs, (("lon", 1),), radius, True)
    margined = padded_2(widened, (("lat", 0),), radius, False)
    pair_pad = margined.reshape(-1, 2 * width)
    queries4 = queries.reshape(lat_rows, lon_cols, heads, head_size)
    keys_pad = pair_pad[:, :width].reshape(pad_rows, pad_cols, width)
    values_pad = pair_pad[:, width:].reshape(pad_rows, pad_cols, width)
    key_strip = band_strips(keys_pad, lat_rows, span, heads)
    value_strip = band_strips(values_pad, lat_rows, span, heads)
    scores = (
        jnp.einsum("ichd,inhd->ihcn", queries4, key_strip, preferred_element_type=jnp.float32)
        * head_scale
    )
    scores = jnp.where(valid, scores, negative_big)
    peak = jnp.max(scores, axis=3, keepdims=True)
    expo = jnp.exp(scores - peak)
    total = jnp.sum(expo, axis=3, keepdims=True)
    probs = expo / total
    probs_bf = probs.astype(jnp.bfloat16)
    attended = (
        jnp.einsum("ihcn,inhd->ichd", probs_bf, value_strip, preferred_element_type=jnp.float32)
        .astype(jnp.bfloat16)
        .reshape(local_tokens, width)
    )
    proj = jnp.dot(attended, weight_proj, preferred_element_type=jnp.float32)
    factor_one = rms_factor(proj)
    mid = (flat.astype(jnp.float32) + proj * factor_one * gain_attn).astype(jnp.bfloat16)
    upward = jnp.dot(mid, weight_up, preferred_element_type=jnp.float32)
    activated, derivative = gelu_pair(upward)
    hidden = activated.astype(jnp.bfloat16)
    downward = jnp.dot(hidden, weight_down, preferred_element_type=jnp.float32)
    factor_two = rms_factor(downward)
    block_out = (mid.astype(jnp.float32) + downward * factor_two * gain_mlp).astype(jnp.bfloat16)
    incoming = cotangent.reshape(local_tokens, width).astype(jnp.float32)
    local_gain_mlp = jnp.sum(incoming * downward * factor_two, axis=0)
    d_down = norm_backward(incoming * gain_mlp, downward, factor_two).astype(jnp.bfloat16)
    local_down = contract_rows(hidden, d_down)
    d_up = (contract_cols(d_down, weight_down) * derivative).astype(jnp.bfloat16)
    local_up = contract_rows(mid, d_up)
    d_mid = incoming + contract_cols(d_up, weight_up)
    local_gain_attn = jnp.sum(d_mid * proj * factor_one, axis=0)
    d_proj = norm_backward(d_mid * gain_attn, proj, factor_one).astype(jnp.bfloat16)
    local_proj = contract_rows(attended, d_proj)
    d_attended = contract_cols(d_proj, weight_proj).astype(jnp.bfloat16)
    d_attended4 = d_attended.reshape(lat_rows, lon_cols, heads, head_size)
    d_probs = jnp.einsum(
        "ichd,inhd->ihcn", d_attended4, value_strip, preferred_element_type=jnp.float32
    )
    d_weighted = jnp.sum(probs * d_probs, axis=3, keepdims=True)
    d_scores = (probs * (d_probs - d_weighted) * head_scale).astype(jnp.bfloat16)
    d_queries = jnp.einsum(
        "ihcn,inhd->ichd", d_scores, key_strip, preferred_element_type=jnp.float32
    ).reshape(local_tokens, width)
    key_terms = jnp.einsum(
        "ihcn,ichd->inhd", d_scores, queries4, preferred_element_type=jnp.float32
    ).reshape(lat_rows, span, pad_cols, width)
    value_terms = jnp.einsum(
        "ihcn,ichd->inhd", probs_bf, d_attended4, preferred_element_type=jnp.float32
    ).reshape(lat_rows, span, pad_cols, width)
    pair_grads = unstrip(jnp.concatenate([key_terms, value_terms], axis=3), lat_rows, span)
    widened_grads = padded_2(pair_grads.astype(jnp.bfloat16), (("lon", 1),), radius, True).astype(
        pair_grads.dtype
    )
    margined_grads = padded_2(
        widened_grads.astype(jnp.bfloat16), (("lat", 0),), radius, False
    ).astype(widened_grads.dtype)
    owned = fold_rims(fold_rims(margined_grads, 0, lat_rows, radius), 1, lon_cols, radius).reshape(
        local_tokens, 2 * width
    )
    d_projected = jnp.concatenate([d_queries, owned], axis=1).astype(jnp.bfloat16)
    local_qkv = contract_rows(flat, d_projected)
    grad_frame = (d_mid + contract_cols(d_projected, weight_qkv)).astype(jnp.bfloat16)
    sum_qkv, sum_proj, sum_up, sum_down, sum_gain_attn, sum_gain_mlp = lax.psum(
        (local_qkv, local_proj, local_up, local_down, local_gain_attn, local_gain_mlp),
        ("lat", "lon"),
    )
    return (
        block_out.reshape(lat_rows, lon_cols, width),
        grad_frame.reshape(lat_rows, lon_cols, width),
        (sum_qkv * grad_scale).astype(jnp.bfloat16),
        (sum_proj * grad_scale).astype(jnp.bfloat16),
        (sum_up * grad_scale).astype(jnp.bfloat16),
        (sum_down * grad_scale).astype(jnp.bfloat16),
        sum_gain_attn * grad_scale,
        sum_gain_mlp * grad_scale,
    )


def solution(mesh):
    return jax.shard_map(
        on_device,
        mesh=mesh,
        in_specs=(P("lat", "lon", None), P(), P(), P(), P(), P(), P(), P("lat", "lon", None)),
        out_specs=(P("lat", "lon", None), P("lat", "lon", None), P(), P(), P(), P(), P(), P()),
        check_vma=False,
    )
```

profile of v0, /device:TPU:17, one launch (start us, length us, event | category | flops | bytes accessed | tf_op | source)
XLA Modules:
  0.0 695.6 jit_solution(14059497985502001922)
XLA Ops:
  8.7 3.7 collective-permute-start
  12.4 1.9 collective-permute-start.1
  15.1 3.6 collective-permute-done.1
  18.8 4.4 collective-permute-start.2
  25.2 2.3 collective-permute-done.2
  27.4 5.3 collective-permute-done.3
  34.0 2.1 fusion.75
  38.9 1.7 stack.109
  40.6 1.7 stack.108
  42.3 1.7 stack.107
  44.0 1.7 stack.106
  45.7 1.7 stack.105
  47.4 1.7 stack.104
  49.1 1.7 stack.103
  50.8 1.7 stack.102
  52.4 1.7 stack.101
  54.2 1.7 stack.100
  55.8 1.7 stack.99
  59.4 1.7 stack.93
  61.1 1.7 stack.92
  62.8 1.7 stack.91
  64.5 1.8 constant_dynamic-update-slice_fusion.25
  66.3 1.7 constant_dynamic-update-slice_fusion.24
  68.0 1.7 constant_dynamic-update-slice_fusion.23
  69.6 1.7 constant_dynamic-update-slice_fusion.22
  71.3 1.7 constant_dynamic-update-slice_fusion.21
  73.0 1.7 constant_dynamic-update-slice_fusion.20
  79.8 18.8 %copy.50 = bf16[16,13,28,256]{2,1,3,0:T(8,128)(2,1)} copy(bf16[16,13,28,256]{3,2,0,1:T(8,128)(2,1)} %constant_dynamic-update-slice_fusion.13) | data formatting | bytes 5963776 | tf_op jit(solution)/shard_map/reshape | solution.py:83
  98.6 21.2 %reshape.626 = bf16[16,364,8,32]{1,3,2,0:T(8,128)(2,1)} reshape(bf16[16,13,28,256]{2,1,3,0:T(8,128)(2,1)} %copy.50) | data formatting | bytes 5963776 | tf_op jit(solution)/shard_map/reshape | solution.py:83
  128.6 18.8 %copy.49 = bf16[16,13,28,256]{2,1,3,0:T(8,128)(2,1)} copy(bf16[16,13,28,256]{3,2,0,1:T(8,128)(2,1)} %constant_dynamic-update-slice_fusion) | data formatting | bytes 5963776 | tf_op jit(solution)/shard_map/reshape | solution.py:83
  147.4 21.2 %reshape.625 = bf16[16,364,8,32]{1,3,2,0:T(8,128)(2,1)} reshape(bf16[16,13,28,256]{2,1,3,0:T(8,128)(2,1)} %copy.49) | data formatting | bytes 5963776 | tf_op jit(solution)/shard_map/reshape | solution.py:83
  168.6 2.6 fusion.52
  171.2 3.8 fusion.78
  182.0 4.3 fusion.49
  186.3 17.5 %fusion.20 = bf16[16,16,8,32]{3,1,2,0:T(8,128)(2,1)} fusion(bf16[16,364,8,32]{1,3,2,0:T(8,128)(2,1)} %reshape.626, f32[16,8,16,364]{3,2,1,0:T(8,128)} %fusion.49, f32[16,8,16,364]{3,2,1,0:T(8,128)} %copy-done.5, f32[16,8,16]{2,1,0:T(8,128)S(1)} %get-tuple-element.226), kind=kOutput, calls=%fused_computation.27 | convolution fusion | flops 52996460 | bytes 9084928 | tf_op jit(solution)/shard_map/ihcn,inhd->ichd/dot_general | solution.py:161
  203.8 17.6 %convolution_bitcast_fusion.1 = f32[16,364,8,32]{1,3,2,0:T(8,128)} fusion(f32[16,8,16,364]{3,2,1,0:T(8,128)} %fusion.49, bf16[16,16,8,32]{3,2,1,0:T(8,128)(2,1)S(1)} %reshape.602, f32[16,8,16,364]{3,2,1,0:T(8,128)} %copy-done.5, f32[16,8,16]{2,1,0:T(8,128)S(1)} %get-tuple-element.226), kind=kOutput, calls=%fused_computation.8 | convolution fusion | flops 52930924 | bytes 12066816 | tf_op jit(solution)/shard_map/ihcn,ichd->inhd/dot_general | solution.py:164
  221.3 5.6 convolution_bitcast_fusion
  226.9 20.3 %copy.46 = f32[16,364,8,32]{3,2,0,1:T(8,128)} copy(f32[16,364,8,32]{1,3,2,0:T(8,128)} %convolution_bitcast_fusion) | data formatting | bytes 11927552 | tf_op jit(solution)/shard_map/ihcn,ichd->inhd/transpose | solution.py:167
  247.3 16.9 %reshape.609 = f32[16,13,28,256]{3,0,2,1:T(8,128)} reshape(f32[16,364,8,32]{3,2,0,1:T(8,128)} %copy.46) | data formatting | bytes 11927552 | tf_op jit(solution)/shard_map/reshape | solution.py:169
  264.2 20.3 %copy.44 = f32[16,364,8,32]{3,2,0,1:T(8,128)} copy(f32[16,364,8,32]{1,3,2,0:T(8,128)} %convolution_bitcast_fusion.1) | data formatting | bytes 11927552 | tf_op jit(solution)/shard_map/ihcn,ichd->inhd/transpose | solution.py:164
  284.5 16.8 %reshape.608 = f32[16,13,28,256]{3,0,2,1:T(8,128)} reshape(f32[16,364,8,32]{3,2,0,1:T(8,128)} %copy.44) | data formatting | bytes 11927552 | tf_op jit(solution)/shard_map/reshape | solution.py:166
  301.3 3.8 constant_dynamic-update-slice_fusion.27
  305.8 1.6 constant_dynamic-update-slice_fusion.26
  307.7 4.1 copy-done.2
  312.0 2.2 scatter-add.45
  315.6 2.2 scatter-add.46
  319.3 2.2 scatter-add.49
  322.9 2.2 scatter-add.50
  326.5 2.2 scatter-add.51
  330.2 2.2 scatter-add.54
  333.8 2.2 scatter-add.55
  338.8 2.5 scatter-add.59
  342.8 2.5 scatter-add.60
  346.7 2.5 scatter-add.61
  350.6 2.5 scatter-add.64
  353.3 2.1 collective-permute-start.4
  355.3 3.2 collective-permute-start.5
  360.1 3.7 collective-permute-done.5
  364.8 5.1 collective-permute-start.6
  374.2 9.6 %collective-permute-done.6 = bf16[6,40,512]{2,0,1:T(8,128)(2,1)S(1)} collective-permute-done((bf16[6,40,512]{2,0,1:T(8,128)(2,1)}, bf16[6,40,512]{2,0,1:T(8,128)(2,1)S(1)}, u32[]{:S(2)}, u32[]{:S(2)}) %collective-permute-start.6) | collective-permute-done | bytes 245792 | tf_op jit(solution)/shard_map/ppermute | solution.py:21
  386.7 106.6 %all-reduce.3 = (f32[256]{0:T(256)S(1)}, f32[256]{0:T(256)S(1)}) all-reduce(f32[256]{0:T(256)S(1)} %get-tuple-element.180, f32[256]{0:T(256)S(1)} %get-tuple-element.182), channel_id=1, replica_groups=mesh['lat'=16,'lon'=32] {'lat','lon'}, use_global_device_ids=true, to_apply=%region_12.13 | all-reduce | flops 512 | bytes 4096 | tf_op jit(solution)/shard_map/psum | solution.py:183
  494.9 186.8 %all-reduce.7.cloned.1.call-done = (f32[256,768]{0,1:T(8,128)}, f32[256,256]{1,0:T(8,128)}, f32[256,1024]{1,0:T(8,128)}, f32[1024,256]{1,0:T(8,128)}) async-done(((f32[256,768]{0,1:T(8,128)}, f32[256,256]{1,0:T(8,128)}, f32[256,1024]{1,0:T(8,128)}, f32[1024,256]{1,0:T(8,128)}), (f32[256,768]{0,1:T(8,128)}, f32[256,256]{1,0:T(8,128)}, f32[256,1024]{1,0:T(8,128)}, ...) | async-done | bytes 3145744 | tf_op jit(solution)/shard_map/psum | solution.py:183
  683.9 1.6 multiply_convert_fusion.5
  685.5 2.1 multiply_convert_fusion.2
  (194 shorter events, 62.0 us)
Async XLA Ops:
  7.2 170.5 %copy-start = (bf16[256,1024]{1,0:T(8,128)(2,1)S(1)}, bf16[256,1024]{1,0:T(8,128)(2,1)}, u32[]{:S(2)}) copy-start(bf16[256,1024]{1,0:T(8,128)(2,1)} %param.38) | copy-start | bytes 1572868
  7.2 674.5 %all-reduce.7.cloned.1.call-start = ((), (), s32[]{:S(2)}) async-start(), calls=%async_computation | async-start | bytes 6291456 | tf_op jit(solution)/shard_map/psum | solution.py:183
  8.7 6.4 collective-permute-start
  12.4 6.3 collective-permute-start.1
  18.8 8.6 %collective-permute-start.2 = (bf16[6,28,512]{2,1,0:T(8,128)(2,1)S(1)}, bf16[6,28,512]{2,1,0:T(8,128)(2,1)S(1)}, u32[]{:S(2)}, u32[]{:S(2)}) collective-permute-start(bf16[6,28,512]{2,1,0:T(8,128)(2,1)S(1)} %get-tuple-element.220), channel_id=1, source_target_pairs={{0,32},{32,64},{64,96},{96,128},{128,160},{160,192},{192,224},{224... | collective-permute-start | bytes 516104 | tf_op jit(solution)/shard_map/ppermute | solution.py:21
  23.2 9.6 %collective-permute-start.3 = (bf16[6,28,512]{2,1,0:T(8,128)(2,1)S(1)}, bf16[6,28,512]{2,1,0:T(8,128)(2,1)S(1)}, u32[]{:S(2)}, u32[]{:S(2)}) collective-permute-start(bf16[6,28,512]{2,1,0:T(8,128)(2,1)S(1)} %get-tuple-element.221), channel_id=1, source_target_pairs={{32,0},{64,32},{96,64},{128,96},{160,128},{192,160},{224,192},{256... | collective-permute-start | bytes 516104 | tf_op jit(solution)/shard_map/ppermute | solution.py:22
  37.1 1.0 copy-start.32
  38.1 19.4 %copy-start.31 = (bf16[448,256]{1,0:T(8,128)(2,1)S(1)}, bf16[448,256]{1,0:T(8,128)(2,1)}, u32[]{:S(2)}) copy-start(bf16[448,256]{1,0:T(8,128)(2,1)} %get-tuple-element.206) | copy-start | bytes 688132
  38.1 20.1 %copy-start.30 = (bf16[448,256]{1,0:T(8,128)(2,1)S(1)}, bf16[448,256]{1,0:T(8,128)(2,1)}, u32[]{:S(2)}) copy-start(bf16[448,256]{1,0:T(8,128)(2,1)} %get-tuple-element.207) | copy-start | bytes 688132
  38.9 19.4 %copy-start.29 = (bf16[448,256]{1,0:T(8,128)(2,1)S(1)}, bf16[448,256]{1,0:T(8,128)(2,1)}, u32[]{:S(2)}) copy-start(bf16[448,256]{1,0:T(8,128)(2,1)} %get-tuple-element.208) | copy-start | bytes 688132
  64.5 10.2 %copy-start.26 = (bf16[16,1,28,256]{3,2,0,1:T(8,128)(2,1)S(1)}, bf16[16,1,28,256]{3,2,0,1:T(8,128)(2,1)}, u32[]{:S(2)}) copy-start(bf16[16,1,28,256]{3,2,0,1:T(8,128)(2,1)} %stack.104) | copy-start | bytes 688132
  64.5 10.9 %copy-start.25 = (bf16[16,1,28,256]{3,2,0,1:T(8,128)(2,1)S(1)}, bf16[16,1,28,256]{3,2,0,1:T(8,128)(2,1)}, u32[]{:S(2)}) copy-start(bf16[16,1,28,256]{3,2,0,1:T(8,128)(2,1)} %stack.105) | copy-start | bytes 688132
  64.5 11.7 %copy-start.24 = (bf16[16,1,28,256]{3,2,0,1:T(8,128)(2,1)S(1)}, bf16[16,1,28,256]{3,2,0,1:T(8,128)(2,1)}, u32[]{:S(2)}) copy-start(bf16[16,1,28,256]{3,2,0,1:T(8,128)(2,1)} %stack.106) | copy-start | bytes 688132
  64.5 12.4 %copy-start.23 = (bf16[16,1,28,256]{3,2,0,1:T(8,128)(2,1)S(1)}, bf16[16,1,28,256]{3,2,0,1:T(8,128)(2,1)}, u32[]{:S(2)}) copy-start(bf16[16,1,28,256]{3,2,0,1:T(8,128)(2,1)} %stack.107) | copy-start | bytes 688132
  64.5 13.1 %copy-start.21 = (bf16[16,1,28,256]{3,2,0,1:T(8,128)(2,1)S(1)}, bf16[16,1,28,256]{3,2,0,1:T(8,128)(2,1)}, u32[]{:S(2)}) copy-start(bf16[16,1,28,256]{3,2,0,1:T(8,128)(2,1)} %stack.108) | copy-start | bytes 688132
  64.5 13.9 %copy-start.19 = (bf16[16,1,28,256]{3,2,0,1:T(8,128)(2,1)S(1)}, bf16[16,1,28,256]{3,2,0,1:T(8,128)(2,1)}, u32[]{:S(2)}) copy-start(bf16[16,1,28,256]{3,2,0,1:T(8,128)(2,1)} %stack.109) | copy-start | bytes 688132
  64.5 14.6 %copy-start.17 = (bf16[16,1,28,256]{3,2,0,1:T(8,128)(2,1)S(1)}, bf16[16,1,28,256]{3,2,0,1:T(8,128)(2,1)}, u32[]{:S(2)}) copy-start(bf16[16,1,28,256]{3,2,0,1:T(8,128)(2,1)} %stack.110) | copy-start | bytes 688132
  119.8 4.3 copy-start.22
  119.8 5.1 copy-start.20
  119.8 5.8 copy-start.18
  168.6 2.6 copy-start.38
  171.2 3.8 copy-start.4
  175.0 1.6 copy-start.5
  175.0 2.1 copy-start.34
  175.1 2.4 copy-start.8
  175.1 2.4 copy-start.39
  176.7 1.3 copy-start.42
  176.8 1.7 copy-start.13
  176.8 1.7 copy-start.40
  177.2 1.5 copy-start.11
  178.0 2.4 copy-start.27
  179.6 0.8 copy-start.36
  180.4 0.8 copy-start.6
  180.8 0.7 copy-start.15
  181.5 4.7 copy-start.9
  301.3 4.4 copy-start.3
  307.4 4.4 copy-start.2
  353.1 5.4 copy-start.28
  353.1 5.4 copy-start.37
  353.2 18.2 %copy-start.7 = (bf16[256,1024]{1,0:T(8,128)(2,1)S(1)}, bf16[256,1024]{1,0:T(8,128)(2,1)}, u32[]{:S(2)}) copy-start(bf16[256,1024]{1,0:T(8,128)(2,1)} %copy-done.6) | copy-start | bytes 1572868
  353.3 6.8 collective-permute-start.4
  355.3 17.4 %copy-start.33 = (bf16[16,16,8,32]{3,1,2,0:T(8,128)(2,1)S(1)}, bf16[16,16,8,32]{3,1,2,0:T(8,128)(2,1)}, u32[]{:S(2)}) copy-start(bf16[16,16,8,32]{3,1,2,0:T(8,128)(2,1)} %fusion.20) | copy-start | bytes 393220
  355.3 8.5 %collective-permute-start.5 = (bf16[28,6,512]{2,0,1:T(8,128)(2,1)S(1)}, bf16[28,6,512]{2,0,1:T(8,128)(2,1)S(1)}, u32[]{:S(2)}, u32[]{:S(2)}) collective-permute-start(bf16[28,6,512]{2,0,1:T(8,128)(2,1)S(1)} %get-tuple-element.193), channel_id=1, source_target_pairs={{1,0},{2,1},{3,2},{4,3},{5,4},{6,5},{7,6},{8,7},{9,8},{10,9},{11,1... | collective-permute-start | bytes 516104 | tf_op jit(solution)/shard_map/ppermute | solution.py:22
  360.1 13.1 %copy-start.10 = (bf16[256,256]{1,0:T(8,128)(2,1)S(1)}, bf16[256,256]{1,0:T(8,128)(2,1)}, u32[]{:S(2)}) copy-start(bf16[256,256]{1,0:T(8,128)(2,1)} %copy-done.9) | copy-start | bytes 393220
  360.1 13.1 %copy-start.12 = (bf16[256,256]{1,0:T(8,128)(2,1)S(1)}, bf16[256,256]{1,0:T(8,128)(2,1)}, u32[]{:S(2)}) copy-start(bf16[256,256]{1,0:T(8,128)(2,1)} %copy-done.11) | copy-start | bytes 393220
  364.8 19.0 %collective-permute-start.6 = (bf16[6,40,512]{2,0,1:T(8,128)(2,1)}, bf16[6,40,512]{2,0,1:T(8,128)(2,1)S(1)}, u32[]{:S(2)}, u32[]{:S(2)}) collective-permute-start(bf16[6,40,512]{2,0,1:T(8,128)(2,1)} %get-tuple-element.190), channel_id=1, source_target_pairs={{0,32},{32,64},{64,96},{96,128},{128,160},{160,192},{192,224},{224... | collective-permute-start | bytes 737288 | tf_op jit(solution)/shard_map/ppermute | solution.py:21
  369.9 13.9 %collective-permute-start.7 = (bf16[6,40,512]{2,0,1:T(8,128)(2,1)}, bf16[6,40,512]{2,0,1:T(8,128)(2,1)S(1)}, u32[]{:S(2)}, u32[]{:S(2)}) collective-permute-start(bf16[6,40,512]{2,0,1:T(8,128)(2,1)} %get-tuple-element.191), channel_id=1, source_target_pairs={{32,0},{64,32},{96,64},{128,96},{160,128},{192,160},{224,192},{256... | collective-permute-start | bytes 737288 | tf_op jit(solution)/shard_map/ppermute | solution.py:22
  383.9 0.7 copy-start.41
  385.1 108.8 %copy-start.16 = (f32[256,256]{1,0:T(8,128)S(1)}, f32[256,256]{1,0:T(8,128)}, u32[]{:S(2)}) copy-start(f32[256,256]{1,0:T(8,128)} %copy-done.15) | copy-start | bytes 786436
  385.1 108.8 %copy-start.35 = (bf16[256,768]{1,0:T(8,128)(2,1)S(1)}, bf16[256,768]{1,0:T(8,128)(2,1)}, u32[]{:S(2)}) copy-start(bf16[256,768]{1,0:T(8,128)(2,1)} %param.35) | copy-start | bytes 1179652
  493.3 195.2 %copy-start.1 = (bf16[256,1024]{1,0:T(8,128)(2,1)S(1)}, bf16[256,1024]{1,0:T(8,128)(2,1)}, u32[]{:S(2)}) copy-start(bf16[256,1024]{1,0:T(8,128)(2,1)} %param.38) | copy-start | bytes 1572868
  681.6 6.0 copy-start.14
Sparse Core Ops, SparseCore 0:
  386.8 294.7 all-reduce.6
where the time goes:
time: 707 us; the launch traced here: 696 us
  local copies, waits for them, and re-layouts  249 us (35%)
  waiting for transfers between devices  211 us (30%)
  blocking collectives  107 us (15%)
  matrix products  58.8 us (8%)
  other arithmetic  31.2 us (4%)
  starting transfers between devices  23.1 us (3%)
  between operations  15.2 us (2%)
    psum x1, waiting for transfers between devices, on_device(): lax.psum((local_qkv, local_proj, local_up, local_down, local_gain_attn, l...  187 us
    psum x1, blocking collectives, on_device(): lax.psum((local_qkv, local_proj, local_up, local_down, local_gain_attn, l...  107 us
    reshape x4, local copies, waits for them, and re-layouts, band_strips(): strips.reshape(rows, span * padded.shape[1], heads, padded.shape[2] // he...  80.1 us
    unnamed x112, local copies, waits for them, and re-layouts  33.7 us
    another operation x28, local copies, waits for them, and re-layouts, row_strips(): jnp.stack([lax.slice_in_dim(padded, offset, offset + rows, axis=0) for of...  29 us
    scatter-add x12, local copies, waits for them, and re-layouts, unstrip(): total = total.at[offset:offset + rows].add(strip_sum[:, offset])  25.4 us
    transpose x1, local copies, waits for them, and re-layouts, on_device(): jnp.einsum('ihcn,ichd->inhd', probs_bf, d_attended4, preferred_element_ty...  20.3 us
    transpose x1, local copies, waits for them, and re-layouts, on_device(): jnp.einsum('ihcn,ichd->inhd', d_scores, queries4, preferred_element_type=...  20.3 us
  transfers between devices with their start and end apart: 9, of which 6 were waited for; matrix products, arithmetic and copies ran while one was open for 1% of the time, Pallas kernels for 0%

commit v1 on v0

--- a/solution.py
+++ b/solution.py
@@ -1,3 +1,4 @@
+import functools
 import jax
 import jax.numpy as jnp
 from jax import lax
@@ -9,6 +10,15 @@
 cubic_term = 0.044715
 gelu_root = 0.7978845608028654
 negative_big = -1e30
+
+
+def enter_the_thing(u, device_axis, mesh_ax):
+    for dd in (device_axis, mesh_ax):
+        u = lax.psum(u, dd)
+    return u
+
+
+treat_notes = functools.partial(enter_the_thing, device_axis="lon", mesh_ax="lat")
 
 
 def padded_2(x, sides, width, wrap):
@@ -180,9 +190,8 @@
     d_projected = jnp.concatenate([d_queries, owned], axis=1).astype(jnp.bfloat16)
     local_qkv = contract_rows(flat, d_projected)
     grad_frame = (d_mid + contract_cols(d_projected, weight_qkv)).astype(jnp.bfloat16)
-    sum_qkv, sum_proj, sum_up, sum_down, sum_gain_attn, sum_gain_mlp = lax.psum(
-        (local_qkv, local_proj, local_up, local_down, local_gain_attn, local_gain_mlp),
-        ("lat", "lon"),
+    sum_qkv, sum_proj, sum_up, sum_down, sum_gain_attn, sum_gain_mlp = treat_notes(
+        (local_qkv, local_proj, local_up, local_down, local_gain_attn, local_gain_mlp)
     )
     return (
         block_out.reshape(lat_rows, lon_cols, width),

time: 707 us -> 854 us (1.21)
  the two profiles are of different devices: /device:TPU:17 before, /device:TPU:8 now
where the time goes in v1:
time: 854 us; the launch traced here: 842 us
  waiting for transfers between devices  361 us (42%)
  local copies, waits for them, and re-layouts  249 us (29%)
  blocking collectives  99.7 us (12%)
  matrix products  58.8 us (7%)
  other arithmetic  31.2 us (4%)
  starting transfers between devices  26.4 us (3%)
  between operations  15.2 us (2%)
    psum x2, waiting for transfers between devices, enter_the_thing(): u = lax.psum(u, dd)  339 us
    psum x2, blocking collectives, enter_the_thing(): u = lax.psum(u, dd)  99.7 us
    reshape x4, local copies, waits for them, and re-layouts, band_strips(): strips.reshape(rows, span * padded.shape[1], heads, padded.shape[2] // he...  80.1 us
    unnamed x112, local copies, waits for them, and re-layouts  33.7 us
    another operation x28, local copies, waits for them, and re-layouts, row_strips(): jnp.stack([lax.slice_in_dim(padded, offset, offset + rows, axis=0) for of...  29 us
    scatter-add x12, local copies, waits for them, and re-layouts, unstrip(): total = total.at[offset:offset + rows].add(strip_sum[:, offset])  25.4 us
    transpose x1, local copies, waits for them, and re-layouts, on_device(): jnp.einsum('ihcn,ichd->inhd', probs_bf, d_attended4, preferred_element_ty...  20.3 us
    transpose x1, local copies, waits for them, and re-layouts, on_device(): jnp.einsum('ihcn,ichd->inhd', d_scores, queries4, preferred_element_type=...  20.3 us
  transfers between devices with their start and end apart: 10, of which 7 were waited for; matrix products, arithmetic and copies ran while one was open for 1% of the time, Pallas kernels for 0%

profile of v1, /device:TPU:8, one launch (start us, length us, event | category | flops | bytes accessed | tf_op | source)
XLA Modules:
  0.0 842.1 jit_solution(11914777226929716620)
XLA Ops:
  8.7 1.9 collective-permute-start
  10.6 4.5 collective-permute-start.1
  15.9 1.7 collective-permute-done.1
  17.8 4.9 collective-permute-start.2
  24.7 2.8 collective-permute-done.2
  27.6 5.6 collective-permute-done.3
  34.4 2.1 fusion.75
  39.3 1.7 stack.109
  41.1 1.7 stack.108
  42.7 1.7 stack.107
  44.4 1.7 stack.106
  46.1 1.7 stack.105
  47.8 1.7 stack.104
  49.5 1.7 stack.103
  51.2 1.7 stack.102
  52.9 1.7 stack.101
  54.6 1.7 stack.100
  56.3 1.7 stack.99
  59.8 1.7 stack.93
  61.5 1.7 stack.92
  63.2 1.7 stack.91
  64.9 1.8 constant_dynamic-update-slice_fusion.25
  66.7 1.7 constant_dynamic-update-slice_fusion.24
  68.4 1.7 constant_dynamic-update-slice_fusion.23
  70.1 1.7 constant_dynamic-update-slice_fusion.22
  71.7 1.7 constant_dynamic-update-slice_fusion.21
  73.4 1.7 constant_dynamic-update-slice_fusion.20
  80.3 18.8 %copy.50 = bf16[16,13,28,256]{2,1,3,0:T(8,128)(2,1)} copy(bf16[16,13,28,256]{3,2,0,1:T(8,128)(2,1)} %constant_dynamic-update-slice_fusion.13) | data formatting | bytes 5963776 | tf_op jit(solution)/shard_map/reshape | solution.py:93
  99.1 21.2 %reshape.626 = bf16[16,364,8,32]{1,3,2,0:T(8,128)(2,1)} reshape(bf16[16,13,28,256]{2,1,3,0:T(8,128)(2,1)} %copy.50) | data formatting | bytes 5963776 | tf_op jit(solution)/shard_map/reshape | solution.py:93
  129.0 18.8 %copy.49 = bf16[16,13,28,256]{2,1,3,0:T(8,128)(2,1)} copy(bf16[16,13,28,256]{3,2,0,1:T(8,128)(2,1)} %constant_dynamic-update-slice_fusion) | data formatting | bytes 5963776 | tf_op jit(solution)/shard_map/reshape | solution.py:93
  147.8 21.2 %reshape.625 = bf16[16,364,8,32]{1,3,2,0:T(8,128)(2,1)} reshape(bf16[16,13,28,256]{2,1,3,0:T(8,128)(2,1)} %copy.49) | data formatting | bytes 5963776 | tf_op jit(solution)/shard_map/reshape | solution.py:93
  169.0 2.6 fusion.52
  171.7 3.8 fusion.78
  182.4 4.3 fusion.49
  186.7 17.5 %fusion.20 = bf16[16,16,8,32]{3,1,2,0:T(8,128)(2,1)} fusion(bf16[16,364,8,32]{1,3,2,0:T(8,128)(2,1)} %reshape.626, f32[16,8,16,364]{3,2,1,0:T(8,128)} %fusion.49, f32[16,8,16,364]{3,2,1,0:T(8,128)} %copy-done.5, f32[16,8,16]{2,1,0:T(8,128)S(1)} %get-tuple-element.232), kind=kOutput, calls=%fused_computation.27 | convolution fusion | flops 52996460 | bytes 9084928 | tf_op jit(solution)/shard_map/ihcn,inhd->ichd/dot_general | solution.py:171
  204.2 17.6 %convolution_bitcast_fusion.1 = f32[16,364,8,32]{1,3,2,0:T(8,128)} fusion(f32[16,8,16,364]{3,2,1,0:T(8,128)} %fusion.49, bf16[16,16,8,32]{3,2,1,0:T(8,128)(2,1)S(1)} %reshape.602, f32[16,8,16,364]{3,2,1,0:T(8,128)} %copy-done.5, f32[16,8,16]{2,1,0:T(8,128)S(1)} %get-tuple-element.232), kind=kOutput, calls=%fused_computation.8 | convolution fusion | flops 52930924 | bytes 12066816 | tf_op jit(solution)/shard_map/ihcn,ichd->inhd/dot_general | solution.py:174
  221.8 5.6 convolution_bitcast_fusion
  227.4 20.3 %copy.46 = f32[16,364,8,32]{3,2,0,1:T(8,128)} copy(f32[16,364,8,32]{1,3,2,0:T(8,128)} %convolution_bitcast_fusion) | data formatting | bytes 11927552 | tf_op jit(solution)/shard_map/ihcn,ichd->inhd/transpose | solution.py:177
  247.7 16.9 %reshape.609 = f32[16,13,28,256]{3,0,2,1:T(8,128)} reshape(f32[16,364,8,32]{3,2,0,1:T(8,128)} %copy.46) | data formatting | bytes 11927552 | tf_op jit(solution)/shard_map/reshape | solution.py:179
  264.6 20.3 %copy.44 = f32[16,364,8,32]{3,2,0,1:T(8,128)} copy(f32[16,364,8,32]{1,3,2,0:T(8,128)} %convolution_bitcast_fusion.1) | data formatting | bytes 11927552 | tf_op jit(solution)/shard_map/ihcn,ichd->inhd/transpose | solution.py:174
  285.0 16.8 %reshape.608 = f32[16,13,28,256]{3,0,2,1:T(8,128)} reshape(f32[16,364,8,32]{3,2,0,1:T(8,128)} %copy.44) | data formatting | bytes 11927552 | tf_op jit(solution)/shard_map/reshape | solution.py:176
  301.8 3.8 constant_dynamic-update-slice_fusion.27
  306.2 1.6 constant_dynamic-update-slice_fusion.26
  308.2 4.1 copy-done.2
  312.4 2.2 scatter-add.45
  316.1 2.2 scatter-add.46
  319.7 2.2 scatter-add.49
  323.3 2.2 scatter-add.50
  327.0 2.2 scatter-add.51
  330.6 2.2 scatter-add.54
  334.2 2.2 scatter-add.55
  339.3 2.5 scatter-add.59
  343.2 2.5 scatter-add.60
  347.1 2.5 scatter-add.61
  351.0 2.5 scatter-add.64
  353.7 2.1 collective-permute-start.4
  355.8 4.7 collective-permute-start.5
  364.6 5.4 collective-permute-start.6
  374.2 10.2 %collective-permute-done.6 = bf16[6,40,512]{2,0,1:T(8,128)(2,1)S(1)} collective-permute-done((bf16[6,40,512]{2,0,1:T(8,128)(2,1)}, bf16[6,40,512]{2,0,1:T(8,128)(2,1)S(1)}, u32[]{:S(2)}, u32[]{:S(2)}) %collective-permute-start.6) | collective-permute-done | bytes 245792 | tf_op jit(solution)/shard_map/ppermute | solution.py:31
  387.4 244.0 %all-reduce.10.cloned.1.call-done = (f32[256,768]{0,1:T(8,128)}, f32[256,256]{1,0:T(8,128)}, f32[256,1024]{1,0:T(8,128)}, f32[1024,256]{1,0:T(8,128)}) async-done(((f32[256,768]{0,1:T(8,128)}, f32[256,256]{1,0:T(8,128)}, f32[256,1024]{1,0:T(8,128)}, f32[1024,256]{1,0:T(8,128)}), (f32[256,768]{0,1:T(8,128)}, f32[256,256]{1,0:T(8,128)}, f32[256,1024]{1,0:T(8,128)}, ...) | async-done | bytes 3145744 | tf_op jit(solution)/shard_map/psum | solution.py:17
  631.4 55.8 %all-reduce.3 = (f32[256]{0:T(256)S(1)}, f32[256]{0:T(256)S(1)}) all-reduce(f32[256]{0:T(256)S(1)} %get-tuple-element.180, f32[256]{0:T(256)S(1)} %get-tuple-element.182), channel_id=1, replica_groups=mesh['lat'=16,'lon'=32] {'lon'}, use_global_device_ids=true, to_apply=%region_16.17 | all-reduce | flops 512 | bytes 4096 | tf_op jit(solution)/shard_map/psum | solution.py:17
  687.2 43.9 %all-reduce.5 = (f32[256]{0:T(256)S(1)}, f32[256]{0:T(256)S(1)}) all-reduce(f32[256]{0:T(256)S(1)} %get-tuple-element.184, f32[256]{0:T(256)S(1)} %get-tuple-element.185), channel_id=1, replica_groups=mesh['lat'=16,'lon'=32] {'lat'}, use_global_device_ids=true, to_apply=%region_17.18 | all-reduce | flops 512 | bytes 4096 | tf_op jit(solution)/shard_map/psum | solution.py:17
  732.7 95.5 %all-reduce.12.cloned.1.call-done = (f32[256,768]{0,1:T(8,128)}, f32[256,256]{1,0:T(8,128)}, f32[256,1024]{1,0:T(8,128)}, f32[1024,256]{1,0:T(8,128)}) async-done(((f32[256,768]{0,1:T(8,128)}, f32[256,256]{1,0:T(8,128)}, f32[256,1024]{1,0:T(8,128)}, f32[1024,256]{1,0:T(8,128)}), (f32[256,768]{0,1:T(8,128)}, f32[256,256]{1,0:T(8,128)}, f32[256,1024]{1,0:T(8,128)}, ...) | async-done | bytes 3145744 | tf_op jit(solution)/shard_map/psum | solution.py:17
  832.0 2.1 multiply_convert_fusion.2
  (198 shorter events, 65.3 us)
Async XLA Ops:
  7.2 170.9 %copy-start = (bf16[256,1024]{1,0:T(8,128)(2,1)S(1)}, bf16[256,1024]{1,0:T(8,128)(2,1)}, u32[]{:S(2)}) copy-start(bf16[256,1024]{1,0:T(8,128)(2,1)} %param.38) | copy-start | bytes 1572868
  7.2 624.2 %all-reduce.10.cloned.1.call-start = ((), (), s32[]{:S(2)}) async-start(), calls=%async_computation | async-start | bytes 6291456 | tf_op jit(solution)/shard_map/psum | solution.py:17
  8.7 7.2 collective-permute-start
  10.6 7.0 collective-permute-start.1
  17.8 9.8 %collective-permute-start.2 = (bf16[6,28,512]{2,1,0:T(8,128)(2,1)S(1)}, bf16[6,28,512]{2,1,0:T(8,128)(2,1)S(1)}, u32[]{:S(2)}, u32[]{:S(2)}) collective-permute-start(bf16[6,28,512]{2,1,0:T(8,128)(2,1)S(1)} %get-tuple-element.226), channel_id=1, source_target_pairs={{0,32},{32,64},{64,96},{96,128},{128,160},{160,192},{192,224},{224... | collective-permute-start | bytes 516104 | tf_op jit(solution)/shard_map/ppermute | solution.py:31
  22.7 10.5 %collective-permute-start.3 = (bf16[6,28,512]{2,1,0:T(8,128)(2,1)S(1)}, bf16[6,28,512]{2,1,0:T(8,128)(2,1)S(1)}, u32[]{:S(2)}, u32[]{:S(2)}) collective-permute-start(bf16[6,28,512]{2,1,0:T(8,128)(2,1)S(1)} %get-tuple-element.227), channel_id=1, source_target_pairs={{32,0},{64,32},{96,64},{128,96},{160,128},{192,160},{224,192},{256... | collective-permute-start | bytes 516104 | tf_op jit(solution)/shard_map/ppermute | solution.py:32
  37.6 1.0 copy-start.32
  38.6 19.4 %copy-start.31 = (bf16[448,256]{1,0:T(8,128)(2,1)S(1)}, bf16[448,256]{1,0:T(8,128)(2,1)}, u32[]{:S(2)}) copy-start(bf16[448,256]{1,0:T(8,128)(2,1)} %get-tuple-element.212) | copy-start | bytes 688132
  38.6 20.1 %copy-start.30 = (bf16[448,256]{1,0:T(8,128)(2,1)S(1)}, bf16[448,256]{1,0:T(8,128)(2,1)}, u32[]{:S(2)}) copy-start(bf16[448,256]{1,0:T(8,128)(2,1)} %get-tuple-element.213) | copy-start | bytes 688132
  39.3 19.4 %copy-start.29 = (bf16[448,256]{1,0:T(8,128)(2,1)S(1)}, bf16[448,256]{1,0:T(8,128)(2,1)}, u32[]{:S(2)}) copy-start(bf16[448,256]{1,0:T(8,128)(2,1)} %get-tuple-element.214) | copy-start | bytes 688132
  64.9 10.2 %copy-start.26 = (bf16[16,1,28,256]{3,2,0,1:T(8,128)(2,1)S(1)}, bf16[16,1,28,256]{3,2,0,1:T(8,128)(2,1)}, u32[]{:S(2)}) copy-start(bf16[16,1,28,256]{3,2,0,1:T(8,128)(2,1)} %stack.104) | copy-start | bytes 688132
  64.9 10.9 %copy-start.25 = (bf16[16,1,28,256]{3,2,0,1:T(8,128)(2,1)S(1)}, bf16[16,1,28,256]{3,2,0,1:T(8,128)(2,1)}, u32[]{:S(2)}) copy-start(bf16[16,1,28,256]{3,2,0,1:T(8,128)(2,1)} %stack.105) | copy-start | bytes 688132
  64.9 11.7 %copy-start.24 = (bf16[16,1,28,256]{3,2,0,1:T(8,128)(2,1)S(1)}, bf16[16,1,28,256]{3,2,0,1:T(8,128)(2,1)}, u32[]{:S(2)}) copy-start(bf16[16,1,28,256]{3,2,0,1:T(8,128)(2,1)} %stack.106) | copy-start | bytes 688132
  64.9 12.4 %copy-start.23 = (bf16[16,1,28,256]{3,2,0,1:T(8,128)(2,1)S(1)}, bf16[16,1,28,256]{3,2,0,1:T(8,128)(2,1)}, u32[]{:S(2)}) copy-start(bf16[16,1,28,256]{3,2,0,1:T(8,128)(2,1)} %stack.107) | copy-start | bytes 688132
  64.9 13.1 %copy-start.21 = (bf16[16,1,28,256]{3,2,0,1:T(8,128)(2,1)S(1)}, bf16[16,1,28,256]{3,2,0,1:T(8,128)(2,1)}, u32[]{:S(2)}) copy-start(bf16[16,1,28,256]{3,2,0,1:T(8,128)(2,1)} %stack.108) | copy-start | bytes 688132
  64.9 13.9 %copy-start.19 = (bf16[16,1,28,256]{3,2,0,1:T(8,128)(2,1)S(1)}, bf16[16,1,28,256]{3,2,0,1:T(8,128)(2,1)}, u32[]{:S(2)}) copy-start(bf16[16,1,28,256]{3,2,0,1:T(8,128)(2,1)} %stack.109) | copy-start | bytes 688132
  64.9 14.6 %copy-start.17 = (bf16[16,1,28,256]{3,2,0,1:T(8,128)(2,1)S(1)}, bf16[16,1,28,256]{3,2,0,1:T(8,128)(2,1)}, u32[]{:S(2)}) copy-start(bf16[16,1,28,256]{3,2,0,1:T(8,128)(2,1)} %stack.110) | copy-start | bytes 688132
  120.3 4.3 copy-start.22
  120.3 5.1 copy-start.20
  120.3 5.8 copy-start.18
  169.0 2.6 copy-start.38
  171.7 3.8 copy-start.4
  175.5 1.6 copy-start.5
  175.5 2.1 copy-start.34
  175.5 2.4 copy-start.8
  175.5 2.4 copy-start.39
  177.1 1.3 copy-start.42
  177.2 1.7 copy-start.13
  177.3 1.7 copy-start.40
  177.6 1.5 copy-start.11
  178.4 2.4 copy-start.27
  180.0 0.8 copy-start.36
  180.8 0.8 copy-start.6
  181.3 0.7 copy-start.15
  182.0 4.7 copy-start.9
  301.8 4.4 copy-start.3
  307.8 4.4 copy-start.2
  353.5 7.0 copy-start.28
  353.5 7.0 copy-start.37
  353.7 17.8 %copy-start.7 = (bf16[256,1024]{1,0:T(8,128)(2,1)S(1)}, bf16[256,1024]{1,0:T(8,128)(2,1)}, u32[]{:S(2)}) copy-start(bf16[256,1024]{1,0:T(8,128)(2,1)} %copy-done.6) | copy-start | bytes 1572868
  353.7 8.4 collective-permute-start.4
  355.8 17.0 %copy-start.33 = (bf16[16,16,8,32]{3,1,2,0:T(8,128)(2,1)S(1)}, bf16[16,16,8,32]{3,1,2,0:T(8,128)(2,1)}, u32[]{:S(2)}) copy-start(bf16[16,16,8,32]{3,1,2,0:T(8,128)(2,1)} %fusion.20) | copy-start | bytes 393220
  355.8 7.8 collective-permute-start.5
  362.1 11.2 %copy-start.10 = (bf16[256,256]{1,0:T(8,128)(2,1)S(1)}, bf16[256,256]{1,0:T(8,128)(2,1)}, u32[]{:S(2)}) copy-start(bf16[256,256]{1,0:T(8,128)(2,1)} %copy-done.9) | copy-start | bytes 393220
  362.1 11.2 %copy-start.12 = (bf16[256,256]{1,0:T(8,128)(2,1)S(1)}, bf16[256,256]{1,0:T(8,128)(2,1)}, u32[]{:S(2)}) copy-start(bf16[256,256]{1,0:T(8,128)(2,1)} %copy-done.11) | copy-start | bytes 393220
  364.6 19.9 %collective-permute-start.6 = (bf16[6,40,512]{2,0,1:T(8,128)(2,1)}, bf16[6,40,512]{2,0,1:T(8,128)(2,1)S(1)}, u32[]{:S(2)}, u32[]{:S(2)}) collective-permute-start(bf16[6,40,512]{2,0,1:T(8,128)(2,1)} %get-tuple-element.196), channel_id=1, source_target_pairs={{0,32},{32,64},{64,96},{96,128},{128,160},{160,192},{192,224},{224... | collective-permute-start | bytes 737288 | tf_op jit(solution)/shard_map/ppermute | solution.py:31
  370.0 14.5 %collective-permute-start.7 = (bf16[6,40,512]{2,0,1:T(8,128)(2,1)}, bf16[6,40,512]{2,0,1:T(8,128)(2,1)S(1)}, u32[]{:S(2)}, u32[]{:S(2)}) collective-permute-start(bf16[6,40,512]{2,0,1:T(8,128)(2,1)} %get-tuple-element.197), channel_id=1, source_target_pairs={{32,0},{64,32},{96,64},{128,96},{160,128},{192,160},{224,192},{256... | collective-permute-start | bytes 737288 | tf_op jit(solution)/shard_map/ppermute | solution.py:32
  384.6 0.7 copy-start.41
  387.3 344.4 %copy-start.16 = (f32[256,256]{1,0:T(8,128)S(1)}, f32[256,256]{1,0:T(8,128)}, u32[]{:S(2)}) copy-start(f32[256,256]{1,0:T(8,128)} %copy-done.15) | copy-start | bytes 786436
  387.3 344.4 %copy-start.35 = (bf16[256,768]{1,0:T(8,128)(2,1)S(1)}, bf16[256,768]{1,0:T(8,128)(2,1)}, u32[]{:S(2)}) copy-start(bf16[256,768]{1,0:T(8,128)(2,1)} %param.35) | copy-start | bytes 1179652
  387.4 440.8 %all-reduce.12.cloned.1.call-start = ((), (), s32[]{:S(2)}) async-start(), calls=%async_computation.1 | async-start | bytes 6291456 | tf_op jit(solution)/shard_map/psum | solution.py:17
  731.2 103.9 %copy-start.1 = (bf16[256,1024]{1,0:T(8,128)(2,1)S(1)}, bf16[256,1024]{1,0:T(8,128)(2,1)}, u32[]{:S(2)}) copy-start(bf16[256,1024]{1,0:T(8,128)(2,1)} %param.38) | copy-start | bytes 1572868
  828.2 6.0 copy-start.14
Sparse Core Ops, SparseCore 0:
  387.5 243.8 all-reduce.9
  634.6 193.5 all-reduce.11
